TPU v7x, 128 devices: a whole 4x4x4 slice. The times are simulated.
128 devices in a mesh: variant: 8 (over z_lo, x), vocab: 16 (over y, z_hi, core).
Axes of the slice: x: 4, y: 4, z: 4 (z_hi: 2, z_lo: 2; z = z_hi * 2 + z_lo), core: 2. Of those that a mesh axis runs over, the one named last changes fastest.
Arguments:
- teacher_hidden: bfloat16 [8, 256, 4096], P(None, None, ('variant', 'vocab')), may hold values from -24 to 24
- teacher_weight: bfloat16 [4096, 64128], P(None, ('vocab', 'variant')), may hold values from -1 to 1
- variant_ids: int32 [8], replicated, may hold values from 0 to 13
- temps: float32 [14], replicated, may hold values from 0.7 to 1.5
- student_hidden: bfloat16 [256, 2048], P(None, 'variant'), may hold values from -24 to 24
- student_weight: bfloat16 [2048, 64128], P('variant', 'vocab'), may hold values from -1 to 1
- token_ids: int32 [256], P('variant'), may hold values from 0 to 64127
- loss_mask: int32 [256], P('variant'), may hold values 0 or 1
Outputs:
- token_loss: float32 [256], P('variant')
- student_grad: float32 [2048, 64128], P('variant', 'vocab')
All inputs are finite; a program needn't handle non-finite values. No bound on the sum of `loss_mask` on one device may be relied on, other than what follows from the above.
Results may differ from a plain program's by a relative error of at most 0.0025.
Values may be sent and summed in bfloat16 or wider, within the bound.
No kernel may reach another device: no remote copies, remote signals or barrier semaphores. Data moves between devices by JAX's collectives and lax.ppermute only.
A program may use at most 192 MiB of HBM per device.

v0:
```python
import jax
import jax.numpy as jnp
from jax import lax
from jax.sharding import PartitionSpec as P

mix_weight = 0.5
loss_scale = 4096.0


def on_device(
    teacher_hidden,
    teacher_weight,
    variant_ids,
    temps,
    student_hidden,
    student_weight,
    token_ids,
    loss_mask,
):
    n_variant = lax.axis_size("variant")
    categories = jnp.arange(temps.shape[0], dtype=jnp.int32)
    taus = jnp.sum(
        jnp.where(variant_ids[:, None] == categories[None, :], temps[None, :], 0.0), axis=1
    )
    hidden_all = lax.all_gather(teacher_hidden, ("variant", "vocab"), axis=2, tiled=True)
    scaled = (
        jnp.einsum("vtd,dc->vtc", hidden_all, teacher_weight, preferred_element_type=jnp.float32)
        / taus[:, None, None]
    )
    local_max = jnp.max(scaled, axis=2)
    top = lax.pmax(local_max, ("variant", "vocab"))
    total = lax.psum(jnp.sum(jnp.exp(scaled - top[:, :, None]), axis=2), ("variant", "vocab"))
    probs = jnp.exp(scaled - top[:, :, None]) / total[:, :, None]
    averaged_cols = jnp.sum(probs, axis=0) / n_variant
    averaged = lax.all_to_all(
        averaged_cols.astype(jnp.bfloat16), "variant", split_axis=0, concat_axis=1, tiled=True
    ).astype(averaged_cols.dtype)
    block = student_hidden
    logits = lax.psum_scatter(
        jnp.dot(block, student_weight, preferred_element_type=jnp.float32),
        "variant",
        scatter_dimension=0,
        tiled=True,
    )
    local_max = jnp.max(logits, axis=1)
    top = lax.pmax(local_max, "vocab")
    total = lax.psum(jnp.sum(jnp.exp(logits - top[:, None]), axis=1), "vocab")
    log_probs = logits - (top + jnp.log(total))[:, None]
    probs_student = jnp.exp(log_probs)
    columns = lax.axis_index("vocab") * logits.shape[1] + jnp.arange(
        logits.shape[1], dtype=jnp.int32
    )
    onehot = token_ids[:, None] == columns[None, :]
    soft, hard = lax.psum(
        (jnp.sum(averaged * log_probs, axis=1), jnp.sum(jnp.where(onehot, log_probs, 0.0), axis=1)),
        "vocab",
    )
    maskf = loss_mask.astype(jnp.float32)
    token_loss = maskf * (-mix_weight * soft - (1.0 - mix_weight) * hard)
    error = (
        loss_scale
        * maskf[:, None]
        * (probs_student - mix_weight * averaged - (1.0 - mix_weight) * onehot.astype(jnp.float32))
    ).astype(jnp.bfloat16)
    block = student_hidden
    student_grad = lax.dot_general(
        block,
        lax.all_gather(error, "variant", axis=0, tiled=True),
        (((0,), (0,)), ((), ())),
        preferred_element_type=jnp.float32,
    )
    return (token_loss, student_grad)


def solution(mesh):
    in_specs = (
        P(None, None, ("variant", "vocab")),
        P(None, ("vocab", "variant")),
        P(),
        P(),
        P(None, "variant"),
        P("variant", "vocab"),
        P("variant"),
        P("variant"),
    )
    out_specs = (P("variant"), P("variant", "vocab"))
    return jax.shard_map(
        on_device, mesh=mesh, in_specs=in_specs, out_specs=out_specs, check_vma=False
    )
```

profile of v0, /device:TPU:0, one launch (start us, length us, event | category | flops | bytes accessed | tf_op | source)
XLA Modules:
  0.0 505.8 jit_solution(16824957268856968234)
XLA Ops:
  8.1 1.5 copy-done
  9.6 3.6 fusion.11
  13.2 0.5 all-gather.3.cloned.1.call-update
  13.8 0.2 select_reduce_fusion
  14.0 60.6 %reduce-scatter.2.cloned.1.call-done = f32[32,4008]{1,0:T(8,128)} async-done(((f32[256,4008]{1,0:T(8,128)}), f32[32,4008]{1,0:T(8,128)}) %reduce-scatter.2.cloned.1.call-update) | async-done | bytes 513040 | tf_op jit(solution)/shard_map/reduce_scatter | solution.py:39
  74.6 1.2 reduce_max.19
  75.8 38.9 %pmax.15 = f32[32]{0:T(128)S(1)} all-reduce(f32[32]{0:T(128)S(1)} %reduce_max.19), channel_id=1, replica_groups=mesh['variant'=8,'vocab'=16] {'vocab'}, use_global_device_ids=true, to_apply=%region_8.9 | all-reduce | flops 32 | bytes 256 | tf_op jit(solution)/shard_map/pmax | solution.py:46
  114.7 151.1 %all-gather.3.cloned.1.call-done = bf16[8,256,4096]{1,2,0:T(8,128)(2,1)} async-done(((bf16[8,256,32]{1,2,0:T(8,128)(2,1)}), bf16[8,256,4096]{1,2,0:T(8,128)(2,1)}) %all-gather.3.cloned.1.call-update) | async-done | bytes 16777232 | tf_op jit(solution)/shard_map/all_gather | solution.py:25
  265.9 14.8 %fusion.10 = (f32[8,256]{1,0:T(8,128)S(1)}, f32[8,256,501]{1,2,0:T(8,128)}) fusion(f32[8]{0:T(128)S(1)} %select_reduce_fusion, bf16[8,256,4096]{1,2,0:T(8,128)(2,1)} %all-gather.3.cloned.1.call-done, bf16[4096,501]{0,1:T(8,128)(2,1)} %param.9), kind=kOutput, calls=%fused_computation.23 | convolution fusion | flops 8407435264 | bytes 24993824 | tf_op jit(solution)/shard_map/vtd,dc->vtc/dot_general | solution.py:27
  280.6 62.0 %pmax.14 = f32[8,256]{1,0:T(8,128)S(1)} all-reduce(f32[8,256]{1,0:T(8,128)S(1)} %get-tuple-element.7), channel_id=1, replica_groups=mesh['variant'=8,'vocab'=16] {'variant','vocab'}, use_global_device_ids=true, to_apply=%region_2.3 | all-reduce | flops 2048 | bytes 16384 | tf_op jit(solution)/shard_map/pmax | solution.py:31
  342.6 2.7 fusion.2
  345.4 64.6 %psum.28 = f32[8,256]{1,0:T(8,128)S(1)} all-reduce(f32[8,256]{1,0:T(8,128)S(1)} %fusion.2), channel_id=1, replica_groups=mesh['variant'=8,'vocab'=16] {'variant','vocab'}, use_global_device_ids=true, to_apply=%region_4.5 | all-reduce | flops 2048 | bytes 16384 | tf_op jit(solution)/shard_map/psum | solution.py:32
  410.0 2.9 divide_reduce_fusion
  413.0 0.8 copy.13
  413.8 3.4 all-to-all-start
  417.3 0.3 exponential_reduce_fusion
  417.6 34.1 %psum.29 = f32[32]{0:T(128)S(1)} all-reduce(f32[32]{0:T(128)S(1)} %exponential_reduce_fusion), channel_id=1, replica_groups=mesh['variant'=8,'vocab'=16] {'vocab'}, use_global_device_ids=true, to_apply=%region_10.11 | all-reduce | flops 32 | bytes 256 | tf_op jit(solution)/shard_map/psum | solution.py:47
  451.8 1.1 copy.14
  452.9 1.4 reshape.27
  454.2 1.1 multiply_reduce_fusion
  455.4 33.7 %all-reduce = (f32[32]{0:T(128)S(1)}, f32[32]{0:T(128)S(1)}) all-reduce(f32[32]{0:T(128)S(1)} %get-tuple-element.3, f32[32]{0:T(128)S(1)} %get-tuple-element.2), channel_id=1, replica_groups=mesh['variant'=8,'vocab'=16] {'vocab'}, use_global_device_ids=true, to_apply=%region_14.15 | all-reduce | flops 64 | bytes 512 | tf_op jit(solution)/shard_map/psum | solution.py:54
  489.1 0.5 subtract_multiply_fusion
  489.6 4.4 all-gather.5.cloned.1.call-done
  494.0 4.3 convolution_bitcast_fusion
  (24 shorter events, 0.3 us)
Async XLA Ops:
  8.0 1.6 copy-start
  8.0 5.8 %copy-start.5 = (f32[14]{0:T(128)S(1)}, f32[14]{0:T(128)}, u32[]{:S(2)}) copy-start(f32[14]{0:T(128)} %param.11) | copy-start | bytes 172
  8.0 5.8 %copy-start.6 = (s32[8]{0:T(128)S(1)}, s32[8]{0:T(128)}, u32[]{:S(2)}) copy-start(s32[8]{0:T(128)} %param.10) | copy-start | bytes 100
  8.0 5.9 %copy-start.4 = (s32[32]{0:T(128)S(1)}, s32[32]{0:T(128)}, u32[]{:S(2)}) copy-start(s32[32]{0:T(128)} %param.15) | copy-start | bytes 388
  8.0 66.6 %reduce-scatter.2.cloned.1.call-start = ((), (), s32[]{:S(2)}) async-start(), calls=%async_computation.3 | async-start | bytes 4718592 | tf_op jit(solution)/shard_map/reduce_scatter | solution.py:39
  13.2 252.7 %all-gather.3.cloned.1.call-start = ((), (), s32[]{:S(2)}) async-start(), calls=%async_computation.2 | async-start | bytes 16908288 | tf_op jit(solution)/shard_map/all_gather | solution.py:25
  345.4 71.9 %copy-start.1 = (f32[32,4008]{1,0:T(8,128)S(1)}, f32[32,4008]{1,0:T(8,128)}, u32[]{:S(2)}) copy-start(f32[32,4008]{1,0:T(8,128)} %reduce-scatter.2.cloned.1.call-done) | copy-start | bytes 1539076
  410.0 44.2 %copy-start.3 = (s32[32]{0:T(128)S(1)}, s32[32]{0:T(128)}, u32[]{:S(2)}) copy-start(s32[32]{0:T(128)} %param.14) | copy-start | bytes 388
  412.9 81.1 %copy-start.2 = (bf16[256,256]{1,0:T(8,128)(2,1)S(1)}, bf16[256,256]{1,0:T(8,128)(2,1)}, u32[]{:S(2)}) copy-start(bf16[256,256]{1,0:T(8,128)(2,1)} %param.12) | copy-start | bytes 393220
  413.8 37.9 %all-to-all-start = ((bf16[8,32,501]{2,1,0:T(8,128)(2,1)}), bf16[8,32,501]{2,1,0:T(8,128)(2,1)S(1)}, u32[]{:S(2)}, u32[]{:S(2)}) async-start(bf16[8,32,501]{2,1,0:T(8,128)(2,1)} %bitcast.1), calls=%async_computation | async-start | bytes 524288 | tf_op jit(solution)/shard_map/all_to_all | solution.py:35
  417.3 76.8 %all-gather.5.cloned.1.call-start = ((), (), s32[]{:S(2)}) async-start(), calls=%async_computation.4 | async-start | bytes 2359296 | tf_op jit(solution)/shard_map/all_gather | solution.py:68
Sparse Core Ops, SparseCore 0:
  13.3 61.2 reduce-scatter.1
  455.5 38.4 all-gather.4
Sparse Core Ops, SparseCore 1:
  15.4 250.4 all-gather.2
where the time goes:
time: 506 us
  blocking collectives  233 us (46%)
  waiting for transfers between devices  217 us (43%)
  matrix products  22.7 us (4%)
  between operations  15.6 us (3%)
  other arithmetic  9.06 us (2%)
    all_gather x1, waiting for transfers between devices, on_device(): lax.all_gather(teacher_hidden, ('variant', 'vocab'), axis=2, tiled=True)  151 us
    psum x1, blocking collectives, on_device(): lax.psum(jnp.sum(jnp.exp(scaled - top[:, :, None]), axis=2), ('variant',...  64.6 us
    pmax x1, blocking collectives, on_device(): top = lax.pmax(local_max, ('variant', 'vocab'))  62 us
    reduce_scatter x1, waiting for transfers between devices, on_device(): lax.psum_scatter(jnp.dot(block, student_weight, preferred_element_type=jn...  60.6 us
    pmax x1, blocking collectives, on_device(): top = lax.pmax(local_max, 'vocab')  38.9 us
    psum x1, blocking collectives, on_device(): total = lax.psum(jnp.sum(jnp.exp(logits - top[:, None]), axis=1), 'vocab')  34.1 us
    psum x1, blocking collectives, on_device(): lax.psum((jnp.sum(averaged * log_probs, axis=1), jnp.sum(jnp.where(onehot...  33.7 us
    dot_general x1, matrix products, on_device(): jnp.einsum('vtd,dc->vtc', hidden_all, teacher_weight, preferred_element_t...  14.8 us
  transfers between devices with their start and end apart: 4, of which 3 were waited for; matrix products, arithmetic and copies ran while one was open for 0% of the time, Pallas kernels for 0%

commit v1 on v0

--- a/solution.py
+++ b/solution.py
@@ -1,3 +1,4 @@
+import functools
 import jax
 import jax.numpy as jnp
 from jax import lax
@@ -5,6 +6,22 @@
 
 mix_weight = 0.5
 loss_scale = 4096.0
+
+
+def lead_page(original, in_dim):
+    tile_out = jnp.concatenate(
+        lax.all_to_all(
+            jnp.stack([original] * lax.axis_size(("variant", "vocab")), axis=0),
+            ("variant", "vocab"),
+            0,
+            0,
+        ),
+        axis=in_dim,
+    )
+    return tile_out
+
+
+hold_the_modes = functools.partial(lead_page, in_dim=2)
 
 
 def on_device(
@@ -22,7 +39,7 @@
     taus = jnp.sum(
         jnp.where(variant_ids[:, None] == categories[None, :], temps[None, :], 0.0), axis=1
     )
-    hidden_all = lax.all_gather(teacher_hidden, ("variant", "vocab"), axis=2, tiled=True)
+    hidden_all = hold_the_modes(teacher_hidden)
     scaled = (
         jnp.einsum("vtd,dc->vtc", hidden_all, teacher_weight, preferred_element_type=jnp.float32)
         / taus[:, None, None]

time: 506 us -> 545 us (1.077)
  blocking collectives: 233 us -> 303 us
  waiting for transfers between devices: 217 us -> 168 us
  local copies, waits for them, and re-layouts: 4.83 us -> 16.6 us
  starting transfers between devices: 3.54 us -> 15.3 us
    all_gather x1 -> x0, waiting for transfers between devices: 151 us -> none  [on_device(): lax.all_gather(teacher_hidden, ('variant', 'vocab'), axis=2, tiled=True)]
    reduce_scatter x1, waiting for transfers between devices: 60.6 us -> 162 us  [on_device(): lax.psum_scatter(jnp.dot(block, student_weight, preferred_element_type=jn...]
    pmax x1, blocking collectives: 38.9 us -> 92.1 us  [on_device(): top = lax.pmax(local_max, 'vocab')]
    pmax x1, blocking collectives: 62 us -> 78.7 us  [on_device(): top = lax.pmax(local_max, ('variant', 'vocab'))]
    all_to_all x0 -> x1, starting transfers between devices: none -> 11.7 us  [lead_page(): lax.all_to_all(jnp.stack([original] * lax.axis_size(('variant', 'vocab'))...]
    all_to_all x0 -> x1, local copies, waits for them, and re-layouts: none -> 8.22 us  [lead_page(): lax.all_to_all(jnp.stack([original] * lax.axis_size(('variant', 'vocab'))...]
    another operation x0 -> x1, local copies, waits for them, and re-layouts: none -> 6.86 us  [lead_page(): jnp.stack([original] * lax.axis_size(('variant', 'vocab')), axis=0)]
  transfers between devices with their start and end apart: 4 -> 4, of which waited for: 3 -> 3; matrix products, arithmetic and copies ran while one was open for 0% -> 1% of each run, Pallas kernels for 0% -> 0%
where the time goes in v1:
time: 545 us; the launch traced here: 544 us
  blocking collectives  303 us (56%)
  waiting for transfers between devices  168 us (31%)
  matrix products  19.1 us (4%)
  local copies, waits for them, and re-layouts  16.6 us (3%)
  starting transfers between devices  15.3 us (3%)
  between operations  14.2 us (3%)
  other arithmetic  9.01 us (2%)
    reduce_scatter x1, waiting for transfers between devices, on_device(): lax.psum_scatter(jnp.dot(block, student_weight, preferred_element_type=jn...  162 us
    pmax x1, blocking collectives, on_device(): top = lax.pmax(local_max, 'vocab')  92.1 us
    pmax x1, blocking collectives, on_device(): top = lax.pmax(local_max, ('variant', 'vocab'))  78.7 us
    psum x1, blocking collectives, on_device(): lax.psum(jnp.sum(jnp.exp(scaled - top[:, :, None]), axis=2), ('variant',...  62.7 us
    psum x1, blocking collectives, on_device(): total = lax.psum(jnp.sum(jnp.exp(logits - top[:, None]), axis=1), 'vocab')  35.3 us
    psum x1, blocking collectives, on_device(): lax.psum((jnp.sum(averaged * log_probs, axis=1), jnp.sum(jnp.where(onehot...  33.6 us
    dot_general x1, matrix products, on_device(): jnp.einsum('vtd,dc->vtc', hidden_all, teacher_weight, preferred_element_t...  12 us
    all_to_all x1, starting transfers between devices, lead_page(): lax.all_to_all(jnp.stack([original] * lax.axis_size(('variant', 'vocab'))...  11.7 us
  transfers between devices with their start and end apart: 4, of which 3 were waited for; matrix products, arithmetic and copies ran while one was open for 1% of the time, Pallas kernels for 0%

profile of v1, /device:TPU:0, one launch (start us, length us, event | category | flops | bytes accessed | tf_op | source)
XLA Modules:
  0.0 544.2 jit_solution(4545162584148173169)
XLA Ops:
  7.2 6.9 %stack.2 = bf16[128,8,256,32]{2,3,1,0:T(8,128)(2,1)} broadcast(bf16[8,256,32]{1,2,0:T(8,128)(2,1)} %param.8), dimensions={1,2,3} | broadcast | bytes 16908288 | tf_op jit(solution)/shard_map/stack | solution.py:14
  14.0 11.7 %all-to-all-start = ((bf16[128,8,256,32]{2,3,1,0:T(8,128)(2,1)}), bf16[128,8,256,32]{2,3,1,0:T(8,128)(2,1)}, u32[]{:S(2)}, u32[]{:S(2)}) async-start(bf16[128,8,256,32]{2,3,1,0:T(8,128)(2,1)} %stack.2), calls=%async_computation | async-start | bytes 33554432 | tf_op jit(solution)/shard_map/all_to_all | solution.py:13
  25.8 2.8 fusion.11
  28.9 161.7 %reduce-scatter.2.cloned.1.call-done = f32[32,4008]{1,0:T(8,128)} async-done(((f32[256,4008]{1,0:T(8,128)}), f32[32,4008]{1,0:T(8,128)}) %reduce-scatter.2.cloned.1.call-update) | async-done | bytes 513040 | tf_op jit(solution)/shard_map/reduce_scatter | solution.py:56
  190.5 1.2 reduce_max.19
  191.7 92.1 %pmax.15 = f32[32]{0:T(128)S(1)} all-reduce(f32[32]{0:T(128)S(1)} %reduce_max.19), channel_id=1, replica_groups=mesh['variant'=8,'vocab'=16] {'vocab'}, use_global_device_ids=true, to_apply=%region_8.9 | all-reduce | flops 32 | bytes 256 | tf_op jit(solution)/shard_map/pmax | solution.py:63
  283.9 1.3 all-to-all-done
  285.2 8.2 %copy.17 = bf16[128,8,256,32]{2,3,0,1:T(8,128)(2,1)S(1)} copy(bf16[128,8,256,32]{2,3,1,0:T(8,128)(2,1)} %all-to-all-done) | data formatting | bytes 33554432 | tf_op jit(solution)/shard_map/all_to_all | solution.py:13
  293.4 12.0 %fusion.10 = (f32[8,256]{1,0:T(8,128)S(1)}, f32[8,256,501]{1,2,0:T(8,128)}) fusion(f32[8]{0:T(128)S(1)} %select_reduce_fusion, bf16[8,256,4096]{1,2,0:T(8,128)(2,1)S(1)} %bitcast.20, bf16[4096,501]{0,1:T(8,128)(2,1)} %param.9), kind=kOutput, calls=%fused_computation.23 | convolution fusion | flops 8407435264 | bytes 24993824 | tf_op jit(solution)/shard_map/vtd,dc->vtc/dot_general | solution.py:44
  305.4 78.7 %pmax.14 = f32[8,256]{1,0:T(8,128)S(1)} all-reduce(f32[8,256]{1,0:T(8,128)S(1)} %get-tuple-element.7), channel_id=1, replica_groups=mesh['variant'=8,'vocab'=16] {'variant','vocab'}, use_global_device_ids=true, to_apply=%region_2.3 | all-reduce | flops 2048 | bytes 16384 | tf_op jit(solution)/shard_map/pmax | solution.py:48
  384.1 2.7 fusion.2
  386.8 62.7 %psum.28 = f32[8,256]{1,0:T(8,128)S(1)} all-reduce(f32[8,256]{1,0:T(8,128)S(1)} %fusion.2), channel_id=1, replica_groups=mesh['variant'=8,'vocab'=16] {'variant','vocab'}, use_global_device_ids=true, to_apply=%region_4.5 | all-reduce | flops 2048 | bytes 16384 | tf_op jit(solution)/shard_map/psum | solution.py:49
  449.6 2.9 divide_reduce_fusion
  452.5 0.8 copy.19
  453.4 3.5 all-to-all-start.1
  457.0 0.3 exponential_reduce_fusion
  457.3 35.3 %psum.29 = f32[32]{0:T(128)S(1)} all-reduce(f32[32]{0:T(128)S(1)} %exponential_reduce_fusion), channel_id=1, replica_groups=mesh['variant'=8,'vocab'=16] {'vocab'}, use_global_device_ids=true, to_apply=%region_10.11 | all-reduce | flops 32 | bytes 256 | tf_op jit(solution)/shard_map/psum | solution.py:64
  492.6 0.3 copy.20
  492.9 0.3 reshape.37
  493.3 1.1 multiply_reduce_fusion
  494.4 33.6 %all-reduce = (f32[32]{0:T(128)S(1)}, f32[32]{0:T(128)S(1)}) all-reduce(f32[32]{0:T(128)S(1)} %get-tuple-element.3, f32[32]{0:T(128)S(1)} %get-tuple-element.2), channel_id=1, replica_groups=mesh['variant'=8,'vocab'=16] {'vocab'}, use_global_device_ids=true, to_apply=%region_14.15 | all-reduce | flops 64 | bytes 512 | tf_op jit(solution)/shard_map/psum | solution.py:71
  528.1 0.5 subtract_multiply_fusion
  528.6 4.5 all-gather.2.cloned.1.call-done
  533.1 4.3 convolution_bitcast_fusion
  (27 shorter events, 0.5 us)
Async XLA Ops:
  7.2 18.7 %copy-start = (bf16[256,4008]{0,1:T(8,128)(2,1)S(1)}, bf16[256,4008]{0,1:T(8,128)(2,1)}, u32[]{:S(2)}) copy-start(bf16[256,4008]{0,1:T(8,128)(2,1)} %param.13) | copy-start | bytes 6156292
  14.0 11.8 %copy-start.3 = (bf16[256,256]{1,0:T(8,128)(2,1)S(1)}, bf16[256,256]{1,0:T(8,128)(2,1)}, u32[]{:S(2)}) copy-start(bf16[256,256]{1,0:T(8,128)(2,1)} %param.12) | copy-start | bytes 393220
  14.0 271.2 %all-to-all-start = ((bf16[128,8,256,32]{2,3,1,0:T(8,128)(2,1)}), bf16[128,8,256,32]{2,3,1,0:T(8,128)(2,1)}, u32[]{:S(2)}, u32[]{:S(2)}) async-start(bf16[128,8,256,32]{2,3,1,0:T(8,128)(2,1)} %stack.2), calls=%async_computation | async-start | bytes 33554432 | tf_op jit(solution)/shard_map/all_to_all | solution.py:13
  25.7 2.9 copy-start.6
  25.7 2.9 copy-start.7
  25.8 3.1 copy-start.5
  25.8 164.8 %reduce-scatter.2.cloned.1.call-start = ((), (), s32[]{:S(2)}) async-start(), calls=%async_computation.3 | async-start | bytes 4718592 | tf_op jit(solution)/shard_map/reduce_scatter | solution.py:56
  386.8 70.1 %copy-start.2 = (f32[32,4008]{1,0:T(8,128)S(1)}, f32[32,4008]{1,0:T(8,128)}, u32[]{:S(2)}) copy-start(f32[32,4008]{1,0:T(8,128)} %reduce-scatter.2.cloned.1.call-done) | copy-start | bytes 1539076
  449.6 43.7 %copy-start.4 = (s32[32]{0:T(128)S(1)}, s32[32]{0:T(128)}, u32[]{:S(2)}) copy-start(s32[32]{0:T(128)} %param.14) | copy-start | bytes 388
  453.4 39.2 %all-to-all-start.1 = ((bf16[8,32,501]{2,1,0:T(8,128)(2,1)}), bf16[8,32,501]{2,1,0:T(8,128)(2,1)S(1)}, u32[]{:S(2)}, u32[]{:S(2)}) async-start(bf16[8,32,501]{2,1,0:T(8,128)(2,1)} %bitcast.3), calls=%async_computation.1 | async-start | bytes 524288 | tf_op jit(solution)/shard_map/all_to_all | solution.py:52
  456.9 76.1 %all-gather.2.cloned.1.call-start = ((), (), s32[]{:S(2)}) async-start(), calls=%async_computation.4 | async-start | bytes 2359296 | tf_op jit(solution)/shard_map/all_gather | solution.py:85
  528.1 9.3 %copy-start.1 = (bf16[256,4008]{0,1:T(8,128)(2,1)S(1)}, bf16[256,4008]{0,1:T(8,128)(2,1)}, u32[]{:S(2)}) copy-start(bf16[256,4008]{0,1:T(8,128)(2,1)} %param.13) | copy-start | bytes 6156292
Sparse Core Ops, SparseCore 0:
  29.0 161.4 reduce-scatter.1
  494.5 38.4 all-gather.1
